TPU v7x, 256 devices: a whole 4x4x8 slice. The times are simulated.
256 devices in a mesh: seq: 128 (over y, x, z), width: 2 (over core).
Axes of the slice: x: 4, y: 4, z: 8, core: 2. Of those that a mesh axis runs over, the one named last changes fastest.
Arguments:
- tokens: bfloat16 [2, 32768, 768], P(None, 'seq', 'width'), may hold values from -6 to 6
- w_in: bfloat16 [768, 3, 768], P(None, None, 'width'), may hold values from -0.21875 to 0.21875
- conv_taps: float32 [3, 3, 768], P(None, None, 'width'), may hold values from -3 to 3
- left_in: bfloat16 [256, 128, 128], P('seq'), may hold values from -0.5 to 0.5
- right_in: bfloat16 [128, 256, 256], P('seq'), may hold values from -0.375 to 0.375
- kernel: bfloat16 [128, 256, 768], P('seq', None, 'width'), may hold values from -6 to 6
- right_out: bfloat16 [128, 256, 256], P('seq'), may hold values from -0.375 to 0.375
- left_out: bfloat16 [256, 128, 128], P('seq'), may hold values from -0.5 to 0.5
- w_out: bfloat16 [768, 768], P('width'), may hold values from -0.21875 to 0.21875
Outputs:
- mixed: bfloat16 [2, 32768, 768], P(None, 'seq', 'width')
All inputs are finite; a program needn't handle non-finite values.
Results may differ from a plain program's by a relative error of at most 0.012.
Values may be sent and summed in bfloat16 or wider, within the bound.
A program may use at most 64 MiB of HBM per device.

v0:
```python
import jax
import jax.numpy as jnp
from jax import lax
from jax.experimental import pallas as pl
from jax.experimental.pallas import tpu as pltpu
from jax.sharding import PartitionSpec as P

BF16 = jnp.bfloat16
F32 = jnp.float32
EDGE = 16
PAD = 8
FIRST = 256


def dot(a, b):
    return jnp.dot(a, b, preferred_element_type=F32)


def spread_rows(count, part):
    rows = lax.broadcasted_iota(jnp.int32, (2 * count, count), 0)
    cols = lax.broadcasted_iota(jnp.int32, (2 * count, count), 1)
    return (rows == 2 * cols + part).astype(BF16)


def spread_cols(count, part):
    rows = lax.broadcasted_iota(jnp.int32, (count, 2 * count), 0)
    cols = lax.broadcasted_iota(jnp.int32, (count, 2 * count), 1)
    return (cols == 2 * rows + part).astype(BF16)


def layer(tok, win, taps, lin, rin, ker, rout, lout, wout, out, recvt,
          tokv, wv, tapv, linv, rinv, kerv, routv, loutv, woutv,
          acc, pad, gate, mix_in, mix_out, send1, recv1, send2, recv2, sendt,
          load_sem, near_send, near_recv, plane_sem, s1, r1, s2, r2, st, rt):
    seq = lax.axis_size("seq")
    me = lax.axis_index("seq")
    w = lax.axis_index("width")
    other = 1 - w
    batch, here, half = tok.shape
    lanes = half // 128
    my, mx, mz = me // 32, (me // 8) % 4, me % 8

    ys = [((my + i) % 4) * 32 for i in range(4)]
    xs = [((mx + i) % 4) * 8 for i in range(4)]
    zs = [(mz + i) % 8 for i in range(8)]

    def away(k):
        return ys[k // 32] + xs[(k // 8) % 4] + zs[k % 8]

    own0 = pl.multiple_of(w * half, half)
    sib0 = pl.multiple_of(other * half, half)
    loads = [
        (tok, tokv.at[:, pl.ds(0, here), pl.ds(0, half)]),
        (win.at[:, pl.ds(own0, half)], wv.at[:, pl.ds(0, half)]),
        (win.at[:, pl.ds(sib0, half)], wv.at[:, pl.ds(half, half)]),
        (taps, tapv),
        (lin, linv),
        (rin, rinv),
        (ker, kerv),
        (rout, routv),
        (lout, loutv),
        (wout.at[:, pl.ds(own0, half)], woutv.at[0]),
        (wout.at[:, pl.ds(sib0, half)], woutv.at[1]),
    ]
    loads = [pltpu.make_async_copy(a, b, load_sem.at[i]) for i, (a, b) in enumerate(loads)]
    for load in loads:
        load.start()

    right, left = (me + 1) % seq, (me + seq - 1) % seq
    barrier = pltpu.get_barrier_semaphore()
    greet = [{"width": other}]
    for s in (right, left):
        greet += [{"seq": s}, {"seq": s, "width": other}]
    greet += [{"seq": away(k)} for k in range(1, 8)]
    greet += [{"seq": away(8 * k)} for k in range(1, 16)]
    for who in greet:
        pl.semaphore_signal(barrier, 1, device_id=who)

    pl.semaphore_wait(barrier, len(greet))
    loads[0].wait()
    near = []
    near.append((tokv.at[:, pl.ds(0, here), pl.ds(0, half)], tokv.at[:, pl.ds(0, here), pl.ds(half, half)], {"width": other}))
    for s, row, to in ((right, here - EDGE, here), (left, 0, here + EDGE)):
        src = tokv.at[:, pl.ds(row, EDGE), pl.ds(0, half)]
        near.append((src, tokv.at[:, pl.ds(to, EDGE), pl.ds(0, half)], {"seq": s}))
        near.append((src, tokv.at[:, pl.ds(to, EDGE), pl.ds(half, half)], {"seq": s, "width": other}))
    near = [
        pltpu.make_async_remote_copy(a, b, near_send.at[i], near_recv.at[i], device_id=who)
        for i, (a, b, who) in enumerate(near)
    ]
    for copy in near:
        copy.start()
    for k in range(1, 8):
        pl.semaphore_signal(plane_sem, 1, device_id={"seq": away(k)})

    loads[1].wait()
    for z in range(batch):
        for j in range(3):
            acc[z, j, :here] = dot(tokv[z, :here, 0:FIRST], wv[j, 0:FIRST, :])

    loads[4].wait()
    loads[8].wait()
    count = linv.shape[1]
    for a in range(2):
        mix_in[:, count * a : count * (a + 1)] = dot(spread_rows(count, a), linv[a]).astype(BF16)
        mix_out[count * a : count * (a + 1), :] = dot(loutv[a], spread_cols(count, a)).astype(BF16)
    loads[2].wait()
    loads[3].wait()
    for copy in near:
        copy.wait_recv()

    edges = jnp.concatenate([tokv[z, here:, 0:FIRST] for z in range(batch)], axis=0)
    for j in range(3):
        part = dot(edges, wv[j, 0:FIRST, :])
        for z in range(batch):
            acc[z, j, here:] = part[2 * EDGE * z : 2 * EDGE * (z + 1)]

    def hops(k):
        return sum(min(i, n - i) for i, n in ((k // 32, 4), (k // 8 % 4, 4), (k % 8, 8)))

    order = sorted(range(1, seq), key=hops, reverse=True)

    def scatter(src, dst, ssem, rsem, z):
        for k in order:
            d = away(k)
            pltpu.make_async_remote_copy(
                src.at[z, :, d], dst.at[z, :, me], ssem.at[z], rsem.at[z], device_id={"seq": d}
            ).start()
        dst[z, :, me] = src[z, :, me]

    def all_of(src, dst, ssem, rsem, z):
        rest = pl.ds(0, seq - 1)
        return pltpu.make_async_remote_copy(
            src.at[z, :, rest], dst.at[z, :, rest], ssem.at[z], rsem.at[z], device_id={"seq": me}
        )

    def put(ref, z, value):
        for l in range(lanes):
            ref[z, l] = value[:, 128 * l : 128 * (l + 1)].reshape(seq, 2, 128)

    def take(ref, z):
        return jnp.concatenate([ref[z, l].reshape(2 * seq, 128) for l in range(lanes)], axis=1)

    first, last = me == 0, me == seq - 1
    for z in range(batch):
        conv = []
        for j in range(3):
            p = acc[z, j] + dot(tokv[z, :, FIRST:], wv[j, FIRST:, :])
            p = p.astype(BF16).astype(F32)
            before = p[here + EDGE - 1 : here + EDGE]
            after = p[here + EDGE : here + EDGE + 1]
            pad[j, PAD - 1 : PAD] = jnp.where(first, 0.0, before)
            pad[j, PAD : PAD + here] = p[:here]
            pad[j, PAD + here : PAD + here + 1] = jnp.where(last, 0.0, after)
            conv.append(
                tapv[0, j : j + 1] * pad[j, PAD - 1 : PAD - 1 + here]
                + tapv[1, j : j + 1] * pad[j, PAD : PAD + here]
                + tapv[2, j : j + 1] * pad[j, PAD + 1 : PAD + 1 + here]
            )
            if j == 0:
                gate[z] = conv[0]
        u = (conv[1] * conv[2]).astype(BF16)
        put(send1, z, dot(mix_in[...], u).astype(BF16))
        if z == 0:
            pl.semaphore_wait(plane_sem, 7)
        scatter(send1, recv1, s1, r1, z)

    loads[5].wait()
    loads[6].wait()
    loads[7].wait()
    for z in range(batch):
        all_of(send1, recv1, s1, r1, z).wait_recv()
        second = dot(rinv[...], take(recv1, z))
        freq = (second * kerv[...].astype(F32)).astype(BF16)
        put(send2, z, dot(routv[...], freq).astype(BF16))
        scatter(send2, recv2, s2, r2, z)

    loads[9].wait()
    loads[10].wait()
    shares = []
    for z in range(batch):
        all_of(send2, recv2, s2, r2, z).wait_recv()
        fourth = dot(mix_out[...], take(recv2, z))
        y = (gate[z] * fourth).astype(BF16)
        sendt[z] = dot(y, woutv[1]).astype(BF16)
        share = pltpu.make_async_remote_copy(
            sendt.at[z], recvt.at[z], st.at[z], rt.at[z], device_id={"width": other}
        )
        share.start()
        own = dot(y, woutv[0])
        share.wait_recv()
        out[z] = own.astype(BF16)
        shares.append(share)

    for copy in near + shares:
        copy.wait_send()
    for z in range(batch):
        all_of(send1, recv1, s1, r1, z).wait_send()
        all_of(send2, recv2, s2, r2, z).wait_send()


def shards(tokens, w_in, conv_taps, left_in, right_in, kernel, right_out, left_out, w_out):
    batch, here, half = tokens.shape
    width = w_in.shape[0]
    seq = lax.axis_size("seq")
    lanes = half // 128
    rows = here + 2 * EDGE
    any_space = pl.BlockSpec(memory_space=pltpu.HBM)
    dma, regular = pltpu.SemaphoreType.DMA, pltpu.SemaphoreType.REGULAR
    exchange = pltpu.VMEM((batch, lanes, seq, 2, 128), BF16)
    args = (tokens, w_in.transpose(1, 0, 2), conv_taps, left_in, right_in[0], kernel[0], right_out[0], left_out, w_out)
    args = tuple(pltpu.with_memory_space_constraint(a, pltpu.HBM) for a in args)
    own, theirs = pl.pallas_call(
        layer,
        out_shape=[jax.ShapeDtypeStruct((batch, here, half), BF16)] * 2,
        in_specs=[any_space] * len(args),
        out_specs=[pl.BlockSpec(memory_space=pltpu.VMEM)] * 2,
        scratch_shapes=[
            pltpu.VMEM((batch, rows, width), BF16),
            pltpu.VMEM((3, width, half), BF16),
            pltpu.VMEM(conv_taps.shape, F32),
            pltpu.VMEM(left_in.shape, BF16),
            pltpu.VMEM(right_in.shape[1:], BF16),
            pltpu.VMEM(kernel.shape[1:], BF16),
            pltpu.VMEM(right_out.shape[1:], BF16),
            pltpu.VMEM(left_out.shape, BF16),
            pltpu.VMEM((2, half, half), BF16),
            pltpu.VMEM((batch, 3, rows, half), F32),
            pltpu.VMEM((3, here + 2 * PAD, half), F32),
            pltpu.VMEM((batch, here, half), F32),
            pltpu.VMEM((here, here), BF16),
            pltpu.VMEM((here, here), BF16),
            exchange, exchange, exchange, exchange,
            pltpu.VMEM((batch, here, half), BF16),
            dma((11,)), dma((5,)), dma((5,)), regular,
            dma((batch,)), dma((batch,)), dma((batch,)), dma((batch,)),
            dma((batch,)), dma((batch,)),
        ],
        compiler_params=pltpu.CompilerParams(collective_id=0, has_side_effects=True, vmem_limit_bytes=24 * 1024 * 1024),
        name="monarch_layer",
    )(*args)
    return (own.astype(F32) + theirs.astype(F32)).astype(BF16)


def solution(mesh):
    in_specs = (
        P(None, "seq", "width"),
        P(None, None, "width"),
        P(None, None, "width"),
        P("seq", None, None),
        P("seq", None, None),
        P("seq", None, "width"),
        P("seq", None, None),
        P("seq", None, None),
        P("width", None),
    )
    out_specs = P(None, "seq", "width")
    return jax.shard_map(shards, mesh=mesh, in_specs=in_specs, out_specs=out_specs, check_vma=False)
```

profile of v0, /device:TPU:1, one launch (start us, length us, event | category | flops | bytes accessed | tf_op | source)
XLA Modules:
  0.0 41.2 jit_solution(6290281807406639844)
XLA Ops:
  0.0 40.3 %monarch_layer.1 = (bf16[2,256,384]{2,1,0:T(8,128)(2,1)S(1)}, bf16[2,256,384]{2,1,0:T(8,128)(2,1)S(1)}) custom-call(bf16[2,256,384]{2,1,0:T(8,128)(2,1)} %tok.1, bf16[3,768,384]{2,1,0:T(8,128)(2,1)} %bitcast.4, f32[3,3,384]{2,1,0:T(4,128)} %taps.1, bf16[2,128,128]{2,1,0:T(8,128)(2,1)} %lin.1, bf16[256,256]{1,0:T(8,128)(2,1)} %bitcast.6, ...), custom_call_target="tpu_custom_call" | custom-call | tf_op jit(solution)/shard_map/monarch_layer/pallas_call | solution.py:213
  40.3 0.8 %add_convert_fusion = bf16[2,256,384]{2,1,0:T(8,128)(2,1)} fusion(bf16[2,256,384]{2,1,0:T(8,128)(2,1)S(1)} %get-tuple-element.8, bf16[2,256,384]{2,1,0:T(8,128)(2,1)S(1)} %get-tuple-element.7), kind=kLoop, calls=%fused_computation | loop fusion | flops 786432 | bytes 1179648 | tf_op jit(solution)/shard_map/convert_element_type | solution.py:242
where the time goes:
time: 41.2 us
  Pallas kernels  40.3 us (98%)
  other arithmetic  0.84 us (2%)
    pallas_call x1, Pallas kernels, shards(): pl.pallas_call(layer, out_shape=[jax.ShapeDtypeStruct((batch, here, half)...  40.3 us
    convert_element_type x1, other arithmetic, shards(): return (own.astype(F32) + theirs.astype(F32)).astype(BF16)  0.84 us

commit v1 on v0

--- a/solution.py
+++ b/solution.py
@@ -40,9 +40,10 @@
     lanes = half // 128
     my, mx, mz = me // 32, (me // 8) % 4, me % 8
 
-    ys = [((my + i) % 4) * 32 for i in range(4)]
-    xs = [((mx + i) % 4) * 8 for i in range(4)]
-    zs = [(mz + i) % 8 for i in range(8)]
+    turn = 1 - 2 * w
+    ys = [((my + 4 + turn * i) % 4) * 32 for i in range(4)]
+    xs = [((mx + 4 + turn * i) % 4) * 8 for i in range(4)]
+    zs = [(mz + 8 + turn * i) % 8 for i in range(8)]
 
     def away(k):
         return ys[k // 32] + xs[(k // 8) % 4] + zs[k % 8]
@@ -120,9 +121,12 @@
 
     order = sorted(range(1, seq), key=hops, reverse=True)
 
-    def scatter(src, dst, ssem, rsem, z):
+    def scatter(src, dst, ssem, rsem, z, early=False):
+        head = jnp.where(me == 0, away(order[0]), 0)
         for k in order:
             d = away(k)
+            if early:
+                d = head if k == order[0] else jnp.where(d == 0, away(order[0]), d)
             pltpu.make_async_remote_copy(
                 src.at[z, :, d], dst.at[z, :, me], ssem.at[z], rsem.at[z], device_id={"seq": d}
             ).start()
@@ -173,10 +177,14 @@
         second = dot(rinv[...], take(recv1, z))
         freq = (second * kerv[...].astype(F32)).astype(BF16)
         put(send2, z, dot(routv[...], freq).astype(BF16))
-        scatter(send2, recv2, s2, r2, z)
+        scatter(send2, recv2, s2, r2, z, z == 1)
 
     loads[9].wait()
     loads[10].wait()
+    for copy in near:
+        copy.wait_send()
+    for z in range(batch):
+        all_of(send1, recv1, s1, r1, z).wait_send()
     shares = []
     for z in range(batch):
         all_of(send2, recv2, s2, r2, z).wait_recv()
@@ -188,15 +196,13 @@
         )
         share.start()
         own = dot(y, woutv[0])
-        share.wait_recv()
         out[z] = own.astype(BF16)
         shares.append(share)
 
-    for copy in near + shares:
-        copy.wait_send()
-    for z in range(batch):
-        all_of(send1, recv1, s1, r1, z).wait_send()
+    for z in range(batch):
         all_of(send2, recv2, s2, r2, z).wait_send()
+    for share in shares:
+        share.wait()
 
 
 def shards(tokens, w_in, conv_taps, left_in, right_in, kernel, right_out, left_out, w_out):

time: 41.2 us -> 39.6 us (0.961)
  Pallas kernels: 40.3 us -> 38.7 us
    pallas_call x1, Pallas kernels: 40.3 us -> 38.7 us  [shards(): pl.pallas_call(layer, out_shape=[jax.ShapeDtypeStruct((batch, here, half)...]
where the time goes in v1:
time: 39.6 us; the launch traced here: 39.5 us
  Pallas kernels  38.7 us (98%)
  other arithmetic  0.84 us (2%)
    pallas_call x1, Pallas kernels, shards(): pl.pallas_call(layer, out_shape=[jax.ShapeDtypeStruct((batch, here, half)...  38.7 us
    convert_element_type x1, other arithmetic, shards(): return (own.astype(F32) + theirs.astype(F32)).astype(BF16)  0.84 us

profile of v1, /device:TPU:1, one launch (start us, length us, event | category | flops | bytes accessed | tf_op | source)
XLA Modules:
  0.0 39.5 jit_solution(15830569946382419685)
XLA Ops:
  0.0 38.7 %monarch_layer.1 = (bf16[2,256,384]{2,1,0:T(8,128)(2,1)S(1)}, bf16[2,256,384]{2,1,0:T(8,128)(2,1)S(1)}) custom-call(bf16[2,256,384]{2,1,0:T(8,128)(2,1)} %tok.1, bf16[3,768,384]{2,1,0:T(8,128)(2,1)} %bitcast.4, f32[3,3,384]{2,1,0:T(4,128)} %taps.1, bf16[2,128,128]{2,1,0:T(8,128)(2,1)} %lin.1, bf16[256,256]{1,0:T(8,128)(2,1)} %bitcast.6, ...), custom_call_target="tpu_custom_call" | custom-call | tf_op jit(solution)/shard_map/monarch_layer/pallas_call | solution.py:219
  38.7 0.8 %add_convert_fusion = bf16[2,256,384]{2,1,0:T(8,128)(2,1)} fusion(bf16[2,256,384]{2,1,0:T(8,128)(2,1)S(1)} %get-tuple-element.8, bf16[2,256,384]{2,1,0:T(8,128)(2,1)S(1)} %get-tuple-element.7), kind=kLoop, calls=%fused_computation | loop fusion | flops 786432 | bytes 1179648 | tf_op jit(solution)/shard_map/convert_element_type | solution.py:248

commit v2 on v1

--- a/solution.py
+++ b/solution.py
@@ -30,7 +30,7 @@
 
 def layer(tok, win, taps, lin, rin, ker, rout, lout, wout, out, recvt,
           tokv, wv, tapv, linv, rinv, kerv, routv, loutv, woutv,
-          acc, pad, gate, mix_in, mix_out, send1, recv1, send2, recv2, sendt,
+          acc, rim, pad, gate, mix_in, mix_out, send1, recv1, send2, recv2, sendt,
           load_sem, near_send, near_recv, plane_sem, s1, r1, s2, r2, st, rt):
     seq = lax.axis_size("seq")
     me = lax.axis_index("seq")
@@ -89,7 +89,7 @@
         pltpu.make_async_remote_copy(a, b, near_send.at[i], near_recv.at[i], device_id=who)
         for i, (a, b, who) in enumerate(near)
     ]
-    for copy in near:
+    for copy in near[1:] + near[:1]:
         copy.start()
     for k in range(1, 8):
         pl.semaphore_signal(plane_sem, 1, device_id={"seq": away(k)})
@@ -97,7 +97,7 @@
     loads[1].wait()
     for z in range(batch):
         for j in range(3):
-            acc[z, j, :here] = dot(tokv[z, :here, 0:FIRST], wv[j, 0:FIRST, :])
+            acc[z, j] = dot(tokv[z, :here, 0:FIRST], wv[j, 0:FIRST, :])
 
     loads[4].wait()
     loads[8].wait()
@@ -107,14 +107,19 @@
         mix_out[count * a : count * (a + 1), :] = dot(loutv[a], spread_cols(count, a)).astype(BF16)
     loads[2].wait()
     loads[3].wait()
-    for copy in near:
+    def rest(z):
+        for j in range(3):
+            whole = acc[z, j] + dot(tokv[z, :here, FIRST:], wv[j, FIRST:, :])
+            pad[z, j, PAD : PAD + here] = whole.astype(BF16).astype(F32)
+
+    near[0].wait_recv()
+    for z in range(batch):
+        rest(z)
+    for copy in near[1:]:
         copy.wait_recv()
-
-    edges = jnp.concatenate([tokv[z, here:, 0:FIRST] for z in range(batch)], axis=0)
+    edges = jnp.concatenate([tokv[z, here:, :] for z in range(batch)], axis=0)
     for j in range(3):
-        part = dot(edges, wv[j, 0:FIRST, :])
-        for z in range(batch):
-            acc[z, j, here:] = part[2 * EDGE * z : 2 * EDGE * (z + 1)]
+        rim[j] = dot(edges, wv[j]).astype(BF16).astype(F32)
 
     def hops(k):
         return sum(min(i, n - i) for i, n in ((k // 32, 4), (k // 8 % 4, 4), (k % 8, 8)))
@@ -149,17 +154,13 @@
     for z in range(batch):
         conv = []
         for j in range(3):
-            p = acc[z, j] + dot(tokv[z, :, FIRST:], wv[j, FIRST:, :])
-            p = p.astype(BF16).astype(F32)
-            before = p[here + EDGE - 1 : here + EDGE]
-            after = p[here + EDGE : here + EDGE + 1]
-            pad[j, PAD - 1 : PAD] = jnp.where(first, 0.0, before)
-            pad[j, PAD : PAD + here] = p[:here]
-            pad[j, PAD + here : PAD + here + 1] = jnp.where(last, 0.0, after)
+            low = 2 * EDGE * z + EDGE - 1
+            pad[z, j, PAD - 1 : PAD] = jnp.where(first, 0.0, rim[j, low : low + 1])
+            pad[z, j, PAD + here : PAD + here + 1] = jnp.where(last, 0.0, rim[j, low + 1 : low + 2])
             conv.append(
-                tapv[0, j : j + 1] * pad[j, PAD - 1 : PAD - 1 + here]
-                + tapv[1, j : j + 1] * pad[j, PAD : PAD + here]
-                + tapv[2, j : j + 1] * pad[j, PAD + 1 : PAD + 1 + here]
+                tapv[0, j : j + 1] * pad[z, j, PAD - 1 : PAD - 1 + here]
+                + tapv[1, j : j + 1] * pad[z, j, PAD : PAD + here]
+                + tapv[2, j : j + 1] * pad[z, j, PAD + 1 : PAD + 1 + here]
             )
             if j == 0:
                 gate[z] = conv[0]
@@ -203,6 +204,17 @@
         all_of(send2, recv2, s2, r2, z).wait_send()
     for share in shares:
         share.wait()
+
+
+def finish(own, theirs, out, total, sem):
+    writes = []
+    for z in range(own.shape[0]):
+        total[z] = (own[z].astype(F32) + theirs[z].astype(F32)).astype(BF16)
+        write = pltpu.make_async_copy(total.at[z], out.at[z], sem.at[z])
+        write.start()
+        writes.append(write)
+    for write in writes:
+        write.wait()
 
 
 def shards(tokens, w_in, conv_taps, left_in, right_in, kernel, right_out, left_out, w_out):
@@ -231,8 +243,9 @@
             pltpu.VMEM(right_out.shape[1:], BF16),
             pltpu.VMEM(left_out.shape, BF16),
             pltpu.VMEM((2, half, half), BF16),
-            pltpu.VMEM((batch, 3, rows, half), F32),
-            pltpu.VMEM((3, here + 2 * PAD, half), F32),
+            pltpu.VMEM((batch, 3, here, half), F32),
+            pltpu.VMEM((3, 2 * EDGE * batch, half), F32),
+            pltpu.VMEM((batch, 3, here + 2 * PAD, half), F32),
             pltpu.VMEM((batch, here, half), F32),
             pltpu.VMEM((here, here), BF16),
             pltpu.VMEM((here, here), BF16),
@@ -245,7 +258,15 @@
         compiler_params=pltpu.CompilerParams(collective_id=0, has_side_effects=True, vmem_limit_bytes=24 * 1024 * 1024),
         name="monarch_layer",
     )(*args)
-    return (own.astype(F32) + theirs.astype(F32)).astype(BF16)
+    return pl.pallas_call(
+        finish,
+        out_shape=jax.ShapeDtypeStruct((batch, here, half), BF16),
+        in_specs=[pl.BlockSpec(memory_space=pltpu.VMEM)] * 2,
+        out_specs=any_space,
+        scratch_shapes=[pltpu.VMEM((batch, here, half), BF16), dma((batch,))],
+        compiler_params=pltpu.CompilerParams(vmem_limit_bytes=4 * 1024 * 1024),
+        name="final_sum",
+    )(own, theirs)
 
 
 def solution(mesh):

time: 39.6 us -> 39.3 us (level)
  other arithmetic: 0.84 us -> 0 us
  Pallas kernels: 38.7 us -> 39.2 us
    convert_element_type x1 -> x0, other arithmetic: 0.84 us -> none  [shards(): return (own.astype(F32) + theirs.astype(F32)).astype(BF16)]
    pallas_call x0 -> x1, Pallas kernels: none -> 0.81 us  [shards(): pl.pallas_call(finish, out_shape=jax.ShapeDtypeStruct((batch, here, half)...]
where the time goes in v2:
time: 39.3 us; the launch traced here: 39.2 us
  Pallas kernels  39.2 us (100%)
    pallas_call x1, Pallas kernels, shards(): pl.pallas_call(layer, out_shape=[jax.ShapeDtypeStruct((batch, here, half)...  38.4 us
    pallas_call x1, Pallas kernels, shards(): pl.pallas_call(finish, out_shape=jax.ShapeDtypeStruct((batch, here, half)...  0.81 us

profile of v2, /device:TPU:1, one launch (start us, length us, event | category | flops | bytes accessed | tf_op | source)
XLA Modules:
  0.0 39.2 jit_solution(18064672848119649244)
XLA Ops:
  0.0 38.4 %monarch_layer.1 = (bf16[2,256,384]{2,1,0:T(8,128)(2,1)S(1)}, bf16[2,256,384]{2,1,0:T(8,128)(2,1)S(1)}) custom-call(bf16[2,256,384]{2,1,0:T(8,128)(2,1)} %tok.1, bf16[3,768,384]{2,1,0:T(8,128)(2,1)} %bitcast.4, f32[3,3,384]{2,1,0:T(4,128)} %taps.1, bf16[2,128,128]{2,1,0:T(8,128)(2,1)} %lin.1, bf16[256,256]{1,0:T(8,128)(2,1)} %bitcast.6, ...), custom_call_target="tpu_custom_call" | custom-call | tf_op jit(solution)/shard_map/monarch_layer/pallas_call | solution.py:231
  38.4 0.8 %final_sum.1 = bf16[2,256,384]{2,1,0:T(8,128)(2,1)} custom-call(bf16[2,256,384]{2,1,0:T(8,128)(2,1)S(1)} %get-tuple-element.7.own, bf16[2,256,384]{2,1,0:T(8,128)(2,1)S(1)} %get-tuple-element.8.theirs), custom_call_target="tpu_custom_call" | custom-call | tf_op jit(solution)/shard_map/final_sum/pallas_call | solution.py:261

commit v3 on v2

--- a/solution.py
+++ b/solution.py
@@ -47,6 +47,17 @@
 
     def away(k):
         return ys[k // 32] + xs[(k // 8) % 4] + zs[k % 8]
+
+    right, left = (me + 1) % seq, (me + seq - 1) % seq
+    barrier = pltpu.get_barrier_semaphore()
+    greet = []
+    for s in (right, left):
+        greet += [{"seq": s}, {"seq": s, "width": other}]
+    greet += [{"seq": away(k)} for k in (4, 3, 5, 2, 6, 1, 7)]
+    greet += [{"seq": away(8 * k)} for k in (10, 6, 9, 11, 14, 5, 7, 13, 15, 2, 8, 1, 3, 4, 12)]
+    greet += [{"width": other}]
+    for who in greet:
+        pl.semaphore_signal(barrier, 1, device_id=who)
 
     own0 = pl.multiple_of(w * half, half)
     sib0 = pl.multiple_of(other * half, half)
@@ -66,16 +77,6 @@
     loads = [pltpu.make_async_copy(a, b, load_sem.at[i]) for i, (a, b) in enumerate(loads)]
     for load in loads:
         load.start()
-
-    right, left = (me + 1) % seq, (me + seq - 1) % seq
-    barrier = pltpu.get_barrier_semaphore()
-    greet = [{"width": other}]
-    for s in (right, left):
-        greet += [{"seq": s}, {"seq": s, "width": other}]
-    greet += [{"seq": away(k)} for k in range(1, 8)]
-    greet += [{"seq": away(8 * k)} for k in range(1, 16)]
-    for who in greet:
-        pl.semaphore_signal(barrier, 1, device_id=who)
 
     pl.semaphore_wait(barrier, len(greet))
     loads[0].wait()

time: 39.3 us -> 39.4 us (level)
  no operation moved by 1% of the time
where the time goes in v3:
time: 39.4 us; the launch traced here: 39.3 us
  Pallas kernels  39.3 us (100%)
    pallas_call x1, Pallas kernels, shards(): pl.pallas_call(layer, out_shape=[jax.ShapeDtypeStruct((batch, here, half)...  38.5 us
    pallas_call x1, Pallas kernels, shards(): pl.pallas_call(finish, out_shape=jax.ShapeDtypeStruct((batch, here, half)...  0.81 us

profile of v3, /device:TPU:1, one launch (start us, length us, event | category | flops | bytes accessed | tf_op | source)
XLA Modules:
  0.0 39.3 jit_solution(6141721668436917562)
XLA Ops:
  0.0 38.5 %monarch_layer.1 = (bf16[2,256,384]{2,1,0:T(8,128)(2,1)S(1)}, bf16[2,256,384]{2,1,0:T(8,128)(2,1)S(1)}) custom-call(bf16[2,256,384]{2,1,0:T(8,128)(2,1)} %tok.1, bf16[3,768,384]{2,1,0:T(8,128)(2,1)} %bitcast.4, f32[3,3,384]{2,1,0:T(4,128)} %taps.1, bf16[2,128,128]{2,1,0:T(8,128)(2,1)} %lin.1, bf16[256,256]{1,0:T(8,128)(2,1)} %bitcast.6, ...), custom_call_target="tpu_custom_call" | custom-call | tf_op jit(solution)/shard_map/monarch_layer/pallas_call | solution.py:232
  38.5 0.8 %final_sum.1 = bf16[2,256,384]{2,1,0:T(8,128)(2,1)} custom-call(bf16[2,256,384]{2,1,0:T(8,128)(2,1)S(1)} %get-tuple-element.7.own, bf16[2,256,384]{2,1,0:T(8,128)(2,1)S(1)} %get-tuple-element.8.theirs), custom_call_target="tpu_custom_call" | custom-call | tf_op jit(solution)/shard_map/final_sum/pallas_call | solution.py:262
